TPU v7x, 256 devices: a whole 4x4x8 slice. The times are simulated.
256 devices in a mesh: role: 2 (over core), dev: 64 (over x_hi, y, z), head: 2 (over x_lo).
Axes of the slice: x: 4 (x_hi: 2, x_lo: 2; x = x_hi * 2 + x_lo), y: 4, z: 8, core: 2. Of those that a mesh axis runs over, the one named last changes fastest.
Arguments:
- hidden: bfloat16 [2048, 4096], P(('role', 'dev', 'head')), may hold values from -6 to 6
- queries: bfloat16 [2048, 64, 128], P(('role', 'dev'), 'head'), as said below
- cache_keys: bfloat16 [2048, 128, 4, 128], P(('role', 'dev'), None, 'head'), as said below
- cache_values: bfloat16 [2048, 128, 4, 128], P(('role', 'dev'), None, 'head'), may hold values from -6 to 6
- new_keys: bfloat16 [2048, 4, 128], P(('role', 'dev'), 'head'), may hold values from -6 to 6
- new_values: bfloat16 [2048, 4, 128], P(('role', 'dev'), 'head'), may hold values from -6 to 6
- lengths: int32 [2048], P(('role', 'dev')), may hold values from 32 to 128, as said below
- out_proj: bfloat16 [8192, 4096], P('head', 'dev'), may hold values from -0.5 to 0.5
- norm_gain: float32 [4096], replicated, may hold values from 0.1 to 1.9
- expert_gate: bfloat16 [128, 4096, 768], P(('role', 'dev'), None, 'head'), may hold values from -0.09375 to 0.09375
- expert_up: bfloat16 [128, 4096, 768], P(('role', 'dev'), None, 'head'), may hold values from -0.09375 to 0.09375
- expert_down: bfloat16 [128, 768, 4096], P(('role', 'dev'), 'head'), may hold values from -0.21875 to 0.21875
- expert_ids: int32 [2048, 8], P(('role', 'dev', 'head')), may hold values from 0 to 127, all different within a row; in each aligned block of 8 rows (0 to 7, 8 to 15, ...) at most 2 rows name the same one
- gate_levels: int32 [2048, 8], P(('role', 'dev', 'head')), may hold values from 1 to 255
Outputs:
- layer_out: bfloat16 [2048, 4096], P(('role', 'dev', 'head'))
Inputs may be any that keep to these rules, and one draw needn't show every extreme that they name: `queries`: query vectors of the new tokens. `cache_keys`: cached keys of the requests. `lengths`: the first request of each block of 16 rows holds 128 positions and the second holds 32. `expert_ids`: each row names 8 different experts; among the 8 rows of one device no expert is named more than 2 times, a bound that some block reaches.
All inputs are finite; a program needn't handle non-finite values.
Results may differ from a plain program's by a relative error of at most 0.0065.
Values may be sent and summed in bfloat16 or wider, within the bound.
No kernel may reach another device: no remote copies, remote signals or barrier semaphores. Data moves between devices by JAX's collectives and lax.ppermute only.
A program may use at most 64 MiB of HBM per device.

v0:
```python
import math
import jax
import jax.numpy as jnp
from jax import lax
from jax.sharding import PartitionSpec as P


def attend_block(query_rows, key_rows, value_rows, key_new, value_new, valid_len):
    row_count = query_rows.shape[0]
    kv_heads = key_rows.shape[2]
    group_size = query_rows.shape[1] // kv_heads
    head_dim = query_rows.shape[2]
    scaling = 1.0 / math.sqrt(head_dim)
    query_f = query_rows.astype(jnp.float32).reshape(row_count, kv_heads, group_size, head_dim)
    scores = jnp.einsum("bhgd,bthd->bhgt", query_f, key_rows.astype(jnp.float32)) * scaling
    scores_new = jnp.einsum("bhgd,bhd->bhg", query_f, key_new.astype(jnp.float32)) * scaling
    positions = jnp.arange(key_rows.shape[1], dtype=jnp.int32)
    usable = (positions[None, :] < valid_len[:, None])[:, None, None, :]
    masked = jnp.where(usable, scores, -1e30)
    highest = jnp.maximum(jnp.max(masked, axis=-1), scores_new)
    exp_terms = jnp.exp(masked - highest[..., None])
    exp_new = jnp.exp(scores_new - highest)
    totals = jnp.sum(exp_terms, axis=-1) + exp_new
    weights = (exp_terms / totals[..., None]).astype(jnp.bfloat16)
    weight_new = (exp_new / totals).astype(jnp.bfloat16)
    blended = jnp.einsum("bhgt,bthd->bhgd", weights, value_rows, preferred_element_type=jnp.float32)
    blended = (
        blended
        + weight_new.astype(jnp.float32)[..., None] * value_new.astype(jnp.float32)[:, :, None, :]
    )
    return blended.astype(jnp.bfloat16).reshape(row_count, kv_heads * group_size * head_dim)


def expert_rows(rows_in, gate_w, up_w, down_w):
    gate_part = jnp.dot(rows_in, gate_w, preferred_element_type=jnp.float32)
    up_part = jnp.dot(rows_in, up_w, preferred_element_type=jnp.float32)
    active = (jax.nn.silu(gate_part) * up_part).astype(jnp.bfloat16)
    return jnp.dot(active, down_w, preferred_element_type=jnp.float32)


def slot_ranks(flat_ids, experts):
    one_hot = (flat_ids[:, None] == jnp.arange(experts, dtype=jnp.int32)[None, :]).astype(jnp.int32)
    return jnp.sum(jnp.cumsum(one_hot, axis=0) * one_hot, axis=1) - 1


def on_device(
    hidden,
    queries,
    cache_keys,
    cache_values,
    new_keys,
    new_values,
    lengths,
    out_proj,
    norm_gain,
    expert_gate,
    expert_up,
    expert_down,
    expert_ids,
    gate_levels,
):
    attended = attend_block(queries, cache_keys, cache_values, new_keys, new_values, lengths)
    columns = jnp.dot(
        lax.all_gather(attended, "dev", axis=0, tiled=True),
        out_proj,
        preferred_element_type=jnp.float32,
    )
    dev_count = lax.axis_size("dev")
    head_count = lax.axis_size("head")
    experts = lax.axis_size("role") * dev_count
    col_width = out_proj.shape[1]
    width = dev_count * col_width
    projected = lax.all_to_all(columns, ("dev", "head"), split_axis=0, concat_axis=1, tiled=True)
    tokens = projected.shape[0]
    summed = jnp.sum(projected.reshape(tokens, dev_count, head_count, col_width), axis=2).reshape(
        tokens, width
    )
    residual = hidden.astype(jnp.float32) + summed
    normed = (
        residual
        * lax.rsqrt(jnp.mean(residual * residual, axis=-1, keepdims=True) + 1e-06)
        * norm_gain
    ).astype(jnp.bfloat16)
    top_k = expert_ids.shape[1]
    capacity = max(2, 2 * tokens * top_k // experts)
    own_ids = expert_ids.reshape(-1)
    own_ranks = slot_ranks(own_ids, experts)
    pair_rows, pair_ids = (
        lax.all_gather(normed, "head", axis=0, tiled=True),
        lax.all_gather(expert_ids, "head", axis=0, tiled=True),
    )
    pair_flat = pair_ids.reshape(head_count, tokens * top_k)
    pair_ranks = jax.vmap(lambda id_row: slot_ranks(id_row, experts))(pair_flat)
    pair_ranks = pair_ranks + capacity * jnp.arange(head_count, dtype=jnp.int32)[:, None]
    rows_from = jnp.arange(head_count * tokens * top_k, dtype=jnp.int32) // top_k
    outgoing = (
        jnp.zeros((experts, head_count * capacity, width), jnp.bfloat16)
        .at[pair_flat.reshape(-1), pair_ranks.reshape(-1)]
        .set(pair_rows[rows_from])
    )
    incoming = lax.all_to_all(outgoing, ("role", "dev"), split_axis=0, concat_axis=0, tiled=True)
    sources = incoming.shape[0]
    slot_total = incoming.shape[1]
    partial_value = expert_rows(
        incoming.reshape(sources * slot_total, width), expert_gate[0], expert_up[0], expert_down[0]
    )
    partial_value = partial_value.reshape(sources, slot_total, width).astype(jnp.bfloat16)
    arrived = lax.all_to_all(
        partial_value, ("role", "dev"), split_axis=0, concat_axis=0, tiled=True
    )
    arrived = (
        lax.psum_scatter(arrived, "head", scatter_dimension=1, tiled=True)
        .astype(jnp.float32)
        .astype(jnp.bfloat16)
    )
    picked = arrived[own_ids, own_ranks].astype(jnp.float32).reshape(tokens, top_k, width)
    levels = gate_levels.astype(jnp.float32)
    shares = levels / jnp.sum(levels, axis=1, keepdims=True)
    return (residual + jnp.sum(shares[..., None] * picked, axis=1)).astype(jnp.bfloat16)


def solution(mesh):
    placed = (
        P(("role", "dev", "head"), None),
        P(("role", "dev"), "head", None),
        P(("role", "dev"), None, "head", None),
        P(("role", "dev"), None, "head", None),
        P(("role", "dev"), "head", None),
        P(("role", "dev"), "head", None),
        P(("role", "dev")),
        P("head", "dev"),
        P(),
        P(("role", "dev"), None, "head"),
        P(("role", "dev"), None, "head"),
        P(("role", "dev"), "head", None),
        P(("role", "dev", "head"), None),
        P(("role", "dev", "head"), None),
    )
    return jax.shard_map(
        on_device,
        mesh=mesh,
        in_specs=placed,
        out_specs=P(("role", "dev", "head"), None),
        check_vma=False,
    )
```

profile of v0, /device:TPU:1, one launch (start us, length us, event | category | flops | bytes accessed | tf_op | source)
XLA Modules:
  0.0 560.9 jit_solution(16563779175409254275)
XLA Ops:
  6.5 0.9 iota_compare_fusion.2
  7.4 1.1 fusion.22
  8.6 2.1 fusion.34
  11.7 1.7 fusion.12
  14.1 3.7 all_gather.10
  18.3 148.0 %all-gather.2.cloned.1.call-done = bf16[1024,4096]{1,0:T(8,128)(2,1)} async-done(((bf16[16,4096]{1,0:T(8,128)(2,1)}), bf16[1024,4096]{1,0:T(8,128)(2,1)}) %all-gather.2.cloned.1.call-update) | async-done | bytes 8388624 | tf_op jit(solution)/shard_map/all_gather | solution.py:64
  166.3 6.6 %convolution_bitcast_fusion = f32[128,8,64]{2,1,0:T(8,128)} fusion(bf16[1024,4096]{1,0:T(8,128)(2,1)} %all-gather.2.cloned.1.call-done, bf16[4096,64]{0,1:T(8,128)(2,1)} %param.21), kind=kOutput, calls=%fused_computation.11 | convolution fusion | flops 536870912 | bytes 9175040 | tf_op jit(solution)/shard_map/dot_general | solution.py:63
  172.9 2.1 reshape.251
  175.0 9.4 %all-to-all-start = ((f32[128,1,512]{2,1,0:T(1,128)}), f32[128,1,512]{2,1,0:T(1,128)S(1)}, u32[]{:S(2)}, u32[]{:S(2)}) async-start(f32[128,1,512]{2,1,0:T(1,128)} %reshape.251), calls=%async_computation | async-start | bytes 524288 | tf_op jit(solution)/shard_map/all_to_all | solution.py:73
  184.8 11.2 %all-to-all-done = f32[128,1,512]{2,1,0:T(1,128)S(1)} async-done(((f32[128,1,512]{2,1,0:T(1,128)}), f32[128,1,512]{2,1,0:T(1,128)S(1)}, u32[]{:S(2)}, u32[]{:S(2)}) %all-to-all-start) | async-done | bytes 262176 | tf_op jit(solution)/shard_map/all_to_all | solution.py:73
  197.2 2.2 reduce
  199.5 0.9 reshape.252
  200.4 1.1 bitcast_reduce_fusion
  201.5 0.7 copy.33
  202.3 1.1 reshape.224
  203.6 3.8 all_gather.11
  207.4 2.2 gather_fusion
  209.5 4.0 broadcast_in_dim.16
  213.6 32.4 %scatter_fusion = bf16[128,4,4096]{2,1,0:T(4,128)(2,1)} fusion(bf16[128,4,4096]{2,1,0:T(4,128)(2,1)} %broadcast_in_dim.16, s32[128]{0:T(128)S(1)} %fusion.32, bf16[128,4096]{1,0:T(8,128)(2,1)} %gather_fusion), kind=kCustom, calls=%fused_computation.2 | custom fusion | bytes 3146752 | tf_op jit(solution)/shard_map/scatter | solution.py:99
  246.0 112.3 %all_to_all.26 = bf16[128,4,4096]{2,1,0:T(4,128)(2,1)} all-to-all(bf16[128,4,4096]{2,1,0:T(4,128)(2,1)} %scatter_fusion), channel_id=1, replica_groups=mesh['role'=2,'dev'=64,'head'=2] {'role','dev'}, dimensions={0} | all-to-all | bytes 8388608 | tf_op jit(solution)/shard_map/all_to_all | solution.py:101
  358.3 6.9 %reshape.225 = bf16[512,4096]{1,0:T(8,128)(2,1)} reshape(bf16[128,4,4096]{2,1,0:T(4,128)(2,1)} %all_to_all.26) | data formatting | bytes 8388608 | tf_op jit(solution)/shard_map/reshape | solution.py:105
  365.2 5.6 %fusion.3 = f32[512,384]{1,0:T(8,128)S(1)} fusion(bf16[512,4096]{1,0:T(8,128)(2,1)} %reshape.225, bf16[1,4096,384]{2,1,0:T(8,128)(2,1)} %param.23), kind=kOutput, calls=%fused_computation.7 | convolution fusion | flops 1610612736 | bytes 8126464 | tf_op jit(solution)/shard_map/dot_general | solution.py:35
  370.8 3.1 fusion.8
  373.9 1.8 dot_general.29
  375.8 3.3 convolution_convert_fusion
  379.1 3.2 copy.35
  382.3 104.9 %all_to_all.27 = bf16[128,4,4096]{2,1,0:T(4,128)(2,1)S(1)} all-to-all(bf16[128,4,4096]{2,1,0:T(4,128)(2,1)S(1)} %copy.35), channel_id=1, replica_groups=mesh['role'=2,'dev'=64,'head'=2] {'role','dev'}, dimensions={0} | all-to-all | bytes 8388608 | tf_op jit(solution)/shard_map/all_to_all | solution.py:108
  487.3 4.2 copy.36
  492.6 50.9 %reduce-scatter.2.cloned.1.call-done = bf16[128,2,4096]{2,0,1:T(8,128)(2,1)} async-done(((bf16[128,4,4096]{2,0,1:T(8,128)(2,1)}), bf16[128,2,4096]{2,0,1:T(8,128)(2,1)}) %reduce-scatter.2.cloned.1.call-update) | async-done | bytes 2097168 | tf_op jit(solution)/shard_map/reduce_scatter | solution.py:112
  543.5 5.1 copy.37
  548.6 3.3 gather_fusion.1
  551.9 1.5 fusion.13
  (49 shorter events, 5.7 us)
Async XLA Ops:
  6.5 369.2 %copy-start = (bf16[1,384,4096]{2,1,0:T(8,128)(2,1)S(1)}, bf16[1,384,4096]{2,1,0:T(8,128)(2,1)}, u32[]{:S(2)}) copy-start(bf16[1,384,4096]{2,1,0:T(8,128)(2,1)} %param.25) | copy-start | bytes 9437188
  6.5 7.6 %copy-start.4 = (s32[8,8]{1,0:T(8,128)S(1)}, s32[8,8]{1,0:T(8,128)}, u32[]{:S(2)}) copy-start(s32[8,8]{1,0:T(8,128)} %param.26) | copy-start | bytes 772
  6.5 159.8 %all-gather.2.cloned.1.call-start = ((), (), s32[]{:S(2)}) async-start(), calls=%async_computation.4 | async-start | bytes 8519680 | tf_op jit(solution)/shard_map/all_gather | solution.py:64
  172.9 30.4 %copy-start.3 = (bf16[8,4096]{1,0:T(8,128)(2,1)S(1)}, bf16[8,4096]{1,0:T(8,128)(2,1)}, u32[]{:S(2)}) copy-start(bf16[8,4096]{1,0:T(8,128)(2,1)} %param.14) | copy-start | bytes 196612
  172.9 30.6 %copy-start.5 = (f32[4096]{0:T(1024)S(1)}, f32[4096]{0:T(1024)}, u32[]{:S(2)}) copy-start(f32[4096]{0:T(1024)} %param.22) | copy-start | bytes 49156
  175.0 21.0 %all-to-all-start = ((f32[128,1,512]{2,1,0:T(1,128)}), f32[128,1,512]{2,1,0:T(1,128)S(1)}, u32[]{:S(2)}, u32[]{:S(2)}) async-start(f32[128,1,512]{2,1,0:T(1,128)} %reshape.251), calls=%async_computation | async-start | bytes 524288 | tf_op jit(solution)/shard_map/all_to_all | solution.py:73
  184.5 359.0 %reduce-scatter.2.cloned.1.call-start = ((), (), s32[]{:S(2)}) async-start(), calls=%async_computation.5 | async-start | bytes 6291456 | tf_op jit(solution)/shard_map/reduce_scatter | solution.py:112
  196.0 0.7 copy-start.2
  365.2 5.6 %copy-start.1 = (bf16[512,4096]{1,0:T(8,128)(2,1)S(1)}, bf16[512,4096]{1,0:T(8,128)(2,1)}, u32[]{:S(2)}) copy-start(bf16[512,4096]{1,0:T(8,128)(2,1)} %reshape.225) | copy-start | bytes 12582916
  365.2 5.6 %copy-start.7 = (bf16[1,4096,384]{2,1,0:T(8,128)(2,1)S(1)}, bf16[1,4096,384]{2,1,0:T(8,128)(2,1)}, u32[]{:S(2)}) copy-start(bf16[1,4096,384]{2,1,0:T(8,128)(2,1)} %param.24) | copy-start | bytes 9437188
  491.5 0.7 copy-start.6
Sparse Core Ops, SparseCore 0:
  14.3 152.0 all-gather.1
  491.6 51.7 reduce-scatter.1
where the time goes:
time: 562 us; the launch traced here: 561 us
  blocking collectives  225 us (40%)
  waiting for transfers between devices  210 us (37%)
  local copies, waits for them, and re-layouts  70.8 us (13%)
  matrix products  23.5 us (4%)
  between operations  13.6 us (2%)
  starting transfers between devices  9.48 us (2%)
  other arithmetic  8.69 us (2%)
    all_gather x1, waiting for transfers between devices, on_device(): lax.all_gather(attended, 'dev', axis=0, tiled=True)  148 us
    all_to_all x1, blocking collectives, on_device(): lax.all_to_all(outgoing, ('role', 'dev'), split_axis=0, concat_axis=0, ti...  112 us
    all_to_all x1, blocking collectives, on_device(): lax.all_to_all(partial_value, ('role', 'dev'), split_axis=0, concat_axis=...  105 us
    reduce_scatter x1, waiting for transfers between devices, on_device(): lax.psum_scatter(arrived, 'head', scatter_dimension=1, tiled=True)  50.9 us
    scatter x1, local copies, waits for them, and re-layouts, on_device(): outgoing = jnp.zeros((experts, head_count * capacity, width), jnp.bfloat1...  32.4 us
  transfers between devices with their start and end apart: 3, of which 3 were waited for; matrix products, arithmetic and copies ran while one was open for 0% of the time, Pallas kernels for 0%

commit v1 on v0

--- a/solution.py
+++ b/solution.py
@@ -3,6 +3,13 @@
 import jax.numpy as jnp
 from jax import lax
 from jax.sharding import PartitionSpec as P
+
+
+def swap_blocks(shard, mesh_axis, split, join):
+    size = lax.axis_size(mesh_axis)
+    tiles = jnp.stack(jnp.split(shard, size, axis=split), axis=0)
+    tiles = lax.all_to_all(tiles, mesh_axis, split_axis=0, concat_axis=0)
+    return jnp.concatenate(tiles, axis=join)
 
 
 def attend_block(query_rows, key_rows, value_rows, key_new, value_new, valid_len):
@@ -70,7 +77,7 @@
     experts = lax.axis_size("role") * dev_count
     col_width = out_proj.shape[1]
     width = dev_count * col_width
-    projected = lax.all_to_all(columns, ("dev", "head"), split_axis=0, concat_axis=1, tiled=True)
+    projected = swap_blocks(columns, ("dev", "head"), 0, 1)
     tokens = projected.shape[0]
     summed = jnp.sum(projected.reshape(tokens, dev_count, head_count, col_width), axis=2).reshape(
         tokens, width

time: 562 us -> 657 us (1.17)
  local copies, waits for them, and re-layouts: 70.8 us -> 164 us
    unnamed x19 -> x145, local copies, waits for them, and re-layouts: 4.77 us -> 93.6 us
where the time goes in v1:
time: 657 us; the launch traced here: 655 us
  blocking collectives  225 us (34%)
  waiting for transfers between devices  210 us (32%)
  local copies, waits for them, and re-layouts  164 us (25%)
  matrix products  23 us (4%)
  between operations  13.6 us (2%)
  other arithmetic  10.1 us (2%)
  starting transfers between devices  10 us (2%)
    all_gather x1, waiting for transfers between devices, on_device(): lax.all_gather(attended, 'dev', axis=0, tiled=True)  148 us
    all_to_all x1, blocking collectives, on_device(): lax.all_to_all(outgoing, ('role', 'dev'), split_axis=0, concat_axis=0, ti...  112 us
    all_to_all x1, blocking collectives, on_device(): lax.all_to_all(partial_value, ('role', 'dev'), split_axis=0, concat_axis=...  105 us
    unnamed x145, local copies, waits for them, and re-layouts  93.6 us
    reduce_scatter x1, waiting for transfers between devices, on_device(): lax.psum_scatter(arrived, 'head', scatter_dimension=1, tiled=True)  50.9 us
    scatter x1, local copies, waits for them, and re-layouts, on_device(): outgoing = jnp.zeros((experts, head_count * capacity, width), jnp.bfloat1...  32.4 us
  transfers between devices with their start and end apart: 3, of which 3 were waited for; matrix products, arithmetic and copies ran while one was open for 0% of the time, Pallas kernels for 0%

profile of v1, /device:TPU:1, one launch (start us, length us, event | category | flops | bytes accessed | tf_op | source)
XLA Modules:
  0.0 655.3 jit_solution(2162875574379702101)
XLA Ops:
  7.4 1.1 fusion.22
  8.6 2.1 fusion.34
  11.7 1.7 fusion.12
  14.1 3.7 all_gather.10
  18.3 148.0 %all-gather.2.cloned.1.call-done = bf16[1024,4096]{1,0:T(8,128)(2,1)} async-done(((bf16[16,4096]{1,0:T(8,128)(2,1)}), bf16[1024,4096]{1,0:T(8,128)(2,1)}) %all-gather.2.cloned.1.call-update) | async-done | bytes 8388624 | tf_op jit(solution)/shard_map/all_gather | solution.py:71
  166.3 6.1 fusion.35
  258.8 3.5 copy.297
  262.3 2.1 reshape.247
  264.4 10.0 %all-to-all-start = ((f32[128,1,512]{2,1,0:T(1,128)}), f32[128,1,512]{2,1,0:T(1,128)}, u32[]{:S(2)}, u32[]{:S(2)}) async-start(f32[128,1,512]{2,1,0:T(1,128)} %reshape.247), calls=%async_computation | async-start | bytes 524288 | tf_op jit(solution)/shard_map/all_to_all | solution.py:11
  274.7 10.8 %all-to-all-done = f32[128,1,512]{2,1,0:T(1,128)} async-done(((f32[128,1,512]{2,1,0:T(1,128)}), f32[128,1,512]{2,1,0:T(1,128)}, u32[]{:S(2)}, u32[]{:S(2)}) %all-to-all-start) | async-done | bytes 262176 | tf_op jit(solution)/shard_map/all_to_all | solution.py:11
  286.0 2.9 reduce
  288.9 1.9 reshape.248
  290.8 1.8 bitcast_reduce_fusion
  292.6 2.9 copy.307
  295.6 2.2 copy.306
  298.0 4.0 all_gather.11
  302.0 2.2 gather_fusion
  304.1 4.0 broadcast_in_dim.16
  308.1 32.4 %scatter_fusion = bf16[128,4,4096]{2,1,0:T(4,128)(2,1)} fusion(bf16[128,4,4096]{2,1,0:T(4,128)(2,1)} %broadcast_in_dim.16, s32[128]{0:T(128)S(1)} %fusion.32, bf16[128,4096]{1,0:T(8,128)(2,1)} %gather_fusion), kind=kCustom, calls=%fused_computation.2 | custom fusion | bytes 3146752 | tf_op jit(solution)/shard_map/scatter | solution.py:106
  340.6 112.1 %all_to_all.15 = bf16[128,4,4096]{2,1,0:T(4,128)(2,1)} all-to-all(bf16[128,4,4096]{2,1,0:T(4,128)(2,1)} %scatter_fusion), channel_id=1, replica_groups=mesh['role'=2,'dev'=64,'head'=2] {'role','dev'}, dimensions={0} | all-to-all | bytes 8388608 | tf_op jit(solution)/shard_map/all_to_all | solution.py:108
  452.7 6.9 %reshape.221 = bf16[512,4096]{1,0:T(8,128)(2,1)} reshape(bf16[128,4,4096]{2,1,0:T(4,128)(2,1)} %all_to_all.15) | data formatting | bytes 8388608 | tf_op jit(solution)/shard_map/reshape | solution.py:112
  459.6 5.6 fusion.3
  465.2 3.1 fusion.8
  468.3 1.8 dot_general.29
  470.2 3.3 convolution_convert_fusion
  473.5 3.2 copy.301
  476.8 104.9 %all_to_all.16 = bf16[128,4,4096]{2,1,0:T(4,128)(2,1)S(1)} all-to-all(bf16[128,4,4096]{2,1,0:T(4,128)(2,1)S(1)} %copy.301), channel_id=1, replica_groups=mesh['role'=2,'dev'=64,'head'=2] {'role','dev'}, dimensions={0} | all-to-all | bytes 8388608 | tf_op jit(solution)/shard_map/all_to_all | solution.py:115
  581.7 4.2 copy.302
  587.0 50.9 %reduce-scatter.2.cloned.1.call-done = bf16[128,2,4096]{2,0,1:T(8,128)(2,1)} async-done(((bf16[128,4,4096]{2,0,1:T(8,128)(2,1)}), bf16[128,2,4096]{2,0,1:T(8,128)(2,1)}) %reduce-scatter.2.cloned.1.call-update) | async-done | bytes 2097168 | tf_op jit(solution)/shard_map/reduce_scatter | solution.py:119
  637.9 5.1 copy.303
  643.0 3.3 gather_fusion.1
  646.4 1.5 fusion.13
  (176 shorter events, 92.2 us)
Async XLA Ops:
  6.5 463.6 %copy-start = (bf16[1,384,4096]{2,1,0:T(8,128)(2,1)S(1)}, bf16[1,384,4096]{2,1,0:T(8,128)(2,1)}, u32[]{:S(2)}) copy-start(bf16[1,384,4096]{2,1,0:T(8,128)(2,1)} %param.25) | copy-start | bytes 9437188
  6.5 7.6 %copy-start.3 = (s32[8,8]{1,0:T(8,128)S(1)}, s32[8,8]{1,0:T(8,128)}, u32[]{:S(2)}) copy-start(s32[8,8]{1,0:T(8,128)} %param.26) | copy-start | bytes 772
  6.5 159.8 %all-gather.2.cloned.1.call-start = ((), (), s32[]{:S(2)}) async-start(), calls=%async_computation.4 | async-start | bytes 8519680 | tf_op jit(solution)/shard_map/all_gather | solution.py:71
  262.3 35.4 %copy-start.2 = (bf16[8,4096]{1,0:T(8,128)(2,1)S(1)}, bf16[8,4096]{1,0:T(8,128)(2,1)}, u32[]{:S(2)}) copy-start(bf16[8,4096]{1,0:T(8,128)(2,1)} %param.14) | copy-start | bytes 196612
  262.3 35.6 %copy-start.4 = (f32[4096]{0:T(1024)S(1)}, f32[4096]{0:T(1024)}, u32[]{:S(2)}) copy-start(f32[4096]{0:T(1024)} %param.22) | copy-start | bytes 49156
  264.4 21.1 %all-to-all-start = ((f32[128,1,512]{2,1,0:T(1,128)}), f32[128,1,512]{2,1,0:T(1,128)}, u32[]{:S(2)}, u32[]{:S(2)}) async-start(f32[128,1,512]{2,1,0:T(1,128)} %reshape.247), calls=%async_computation | async-start | bytes 524288 | tf_op jit(solution)/shard_map/all_to_all | solution.py:11
  274.4 363.5 %reduce-scatter.2.cloned.1.call-start = ((), (), s32[]{:S(2)}) async-start(), calls=%async_computation.5 | async-start | bytes 6291456 | tf_op jit(solution)/shard_map/reduce_scatter | solution.py:119
  459.6 5.6 copy-start.1
  459.6 5.6 copy-start.6
  585.9 0.7 copy-start.5
Sparse Core Ops, SparseCore 0:
  14.3 152.0 all-gather.1
  586.1 51.7 reduce-scatter.1
